TPU v7x, 256 devices: a whole 4x4x8 slice. The times are simulated.
256 devices in a mesh: worker: 16 (over y, z_lo, core), expert: 16 (over z_hi, x).
Axes of the slice: x: 4, y: 4, z: 8 (z_hi: 4, z_lo: 2; z = z_hi * 2 + z_lo), core: 2. Of those that a mesh axis runs over, the one named last changes fastest.
Arguments:
- tokens: bfloat16 [32768, 3072], P(('worker', 'expert')), may hold values from -6 to 6
- route_ids: int32 [32768, 2], P(('worker', 'expert')), may hold values from 0 to 3, as said below
- route_mix: float32 [32768, 2], P(('worker', 'expert')), may hold values from 0.1 to 1
- target: bfloat16 [32768, 3072], P(('worker', 'expert')), may hold values from -6 to 6
- step_count: int32 [16], P('worker'), may hold values from 8 to 101
- gate_weight: bfloat16 [3072, 4096], P(None, 'expert'), may hold values from -0.109375 to 0.109375
- up_weight: bfloat16 [3072, 4096], P(None, 'expert'), may hold values from -0.109375 to 0.109375
- down_weight: bfloat16 [4096, 3072], P('expert'), may hold values from -0.1875 to 0.1875
Outputs:
- outer_gate: float32 [3072, 4096], P('worker', 'expert')
- outer_up: float32 [3072, 4096], P('worker', 'expert')
- outer_down: float32 [4096, 3072], P('expert', 'worker')
- token_loss: float32 [32768], P(('worker', 'expert'))
Inputs may be any that keep to these rules, and one draw needn't show every extreme that they name: `route_ids`: each token's 2 experts differ. In the 128 rows of one device no expert is named by more than 80 rows, and in every device's rows some expert is named by exactly 80.
All inputs are finite; a program needn't handle non-finite values.
Results may differ from a plain program's by a relative error of at most 0.017.
Values may be sent and summed in bfloat16 or wider, within the bound.
A program may use at most 128 MiB of HBM per device.

v0:
```python
import jax
import jax.numpy as jnp
from jax import lax
from jax.sharding import PartitionSpec as P

EXPERTS = 4
CAP = 80


def silu_parts(pre):
    sigmoid_val = jax.nn.sigmoid(pre)
    return (pre * sigmoid_val, sigmoid_val * (1.0 + pre * (1.0 - sigmoid_val)))


def contract_rows(left, right):
    return lax.dot_general(
        left, right, (((0,), (0,)), ((), ())), preferred_element_type=jnp.float32
    )


def expert_forward(inputs, gate_weight, up_weight, down_weight):
    gate_pre = jnp.dot(inputs, gate_weight, preferred_element_type=jnp.float32)
    up_pre = jnp.dot(inputs, up_weight, preferred_element_type=jnp.float32)
    hidden = (gate_pre * jax.nn.sigmoid(gate_pre) * up_pre).astype(jnp.bfloat16)
    partial_out = jnp.dot(hidden, down_weight, preferred_element_type=jnp.float32).astype(
        jnp.bfloat16
    )
    return (gate_pre, up_pre, hidden, partial_out)


def hidden_grads(cotangent, gate_pre, up_pre, down_weight):
    grad_hidden = lax.dot_general(
        cotangent, down_weight, (((1,), (1,)), ((), ())), preferred_element_type=jnp.float32
    )
    activated, slope = silu_parts(gate_pre)
    return (
        (grad_hidden * up_pre * slope).astype(jnp.bfloat16),
        (grad_hidden * activated).astype(jnp.bfloat16),
    )


def per_device(
    tokens, route_ids, route_mix, target, step_count, gate_weight, up_weight, down_weight
):
    tok_dev, width = tokens.shape
    topk = route_ids.shape[1]
    route_total = tok_dev * topk
    expert_devices = lax.axis_size("expert")
    hsplit = expert_devices // EXPERTS
    slot_total = expert_devices * CAP
    flat_ids = route_ids.reshape(-1)
    expert_hit = (flat_ids[:, None] == jnp.arange(EXPERTS, dtype=jnp.int32)[None, :]).astype(
        jnp.int32
    )
    earlier = jnp.cumsum(expert_hit, axis=0) - expert_hit
    slot_index = jnp.sum(earlier * expert_hit, axis=1)
    slot_key = flat_ids * CAP + slot_index
    route_of_slot = (
        jnp.full((EXPERTS * CAP,), route_total, jnp.int32)
        .at[slot_key]
        .set(jnp.arange(route_total, dtype=jnp.int32))
    )
    send_live = route_of_slot < route_total
    safe_route = jnp.minimum(route_of_slot, route_total - 1)
    token_picked = jnp.take(tokens, safe_route // topk, axis=0)
    dispatch_one = jnp.where(
        send_live[:, None], token_picked, jnp.zeros_like(token_picked)
    ).reshape(EXPERTS, CAP, width)
    send_tokens = jnp.broadcast_to(dispatch_one[:, None], (EXPERTS, hsplit, CAP, width)).reshape(
        expert_devices, CAP, width
    )
    arrived = lax.all_to_all(send_tokens, "expert", split_axis=0, concat_axis=0, tiled=True)
    expert_rows = arrived.reshape(slot_total, width)
    gate_pre, up_pre, hidden, partial_slots = expert_forward(
        expert_rows, gate_weight, up_weight, down_weight
    )
    returned = lax.all_to_all(
        partial_slots.reshape(expert_devices, CAP, width),
        "expert",
        split_axis=0,
        concat_axis=0,
        tiled=True,
    )
    expert_out = jnp.sum(
        returned.reshape(EXPERTS, hsplit, CAP, width).astype(jnp.float32), axis=1
    ).reshape(EXPERTS * CAP, width)
    picked_rows = jnp.take(expert_out, slot_key, axis=0).reshape(tok_dev, topk, width)
    mixed_out = jnp.sum(route_mix[:, :, None] * picked_rows, axis=1)
    residual = mixed_out - target.astype(jnp.float32)
    token_loss = 0.5 * jnp.mean(residual * residual, axis=1)
    cot_routes = (
        (route_mix[:, :, None] * residual[:, None, :])
        .astype(jnp.bfloat16)
        .reshape(route_total, width)
    )
    cot_picked = jnp.take(cot_routes, safe_route, axis=0)
    cot_one = jnp.where(send_live[:, None], cot_picked, jnp.zeros_like(cot_picked)).reshape(
        EXPERTS, CAP, width
    )
    send_cot = jnp.broadcast_to(cot_one[:, None], (EXPERTS, hsplit, CAP, width)).reshape(
        expert_devices, CAP, width
    )
    cot_arrived = lax.all_to_all(send_cot, "expert", split_axis=0, concat_axis=0, tiled=True)
    cot_slots = cot_arrived.reshape(slot_total, width)
    weight = step_count[0].astype(jnp.float32)
    total_steps = lax.psum(weight, "worker")
    grad_gate, grad_up = hidden_grads(cot_slots, gate_pre, up_pre, down_weight)
    down_grad, grad_gate, grad_up = (contract_rows(hidden, cot_slots), grad_gate, grad_up)
    gate_grad = contract_rows(expert_rows, grad_gate)
    up_grad = contract_rows(expert_rows, grad_up)
    outer_gate, outer_up, outer_down = (
        lax.psum_scatter(
            (weight * gate_grad).astype(jnp.bfloat16), "worker", scatter_dimension=0, tiled=True
        ).astype(jnp.float32),
        lax.psum_scatter(
            (weight * up_grad).astype(jnp.bfloat16), "worker", scatter_dimension=0, tiled=True
        ).astype(jnp.float32),
        lax.psum_scatter(
            (weight * down_grad).astype(jnp.bfloat16), "worker", scatter_dimension=1, tiled=True
        ).astype(jnp.float32),
    )
    return (outer_gate / total_steps, outer_up / total_steps, outer_down / total_steps, token_loss)


def solution(mesh):
    return jax.shard_map(
        per_device,
        mesh=mesh,
        in_specs=(
            P(("worker", "expert"), None),
            P(("worker", "expert"), None),
            P(("worker", "expert"), None),
            P(("worker", "expert"), None),
            P("worker"),
            P(None, "expert"),
            P(None, "expert"),
            P("expert", None),
        ),
        out_specs=(
            P("worker", "expert"),
            P("worker", "expert"),
            P("expert", "worker"),
            P(("worker", "expert")),
        ),
        check_vma=False,
    )
```

profile of v0, /device:TPU:4, one launch (start us, length us, event | category | flops | bytes accessed | tf_op | source)
XLA Modules:
  0.0 849.6 jit_solution(9377517444615883189)
XLA Ops:
  9.1 1.2 reduce-window.6
  11.0 1.4 scatter_custom_fusion
  14.1 7.3 gather_fusion
  23.4 186.5 %all_to_all.15 = bf16[16,80,3072]{2,1,0:T(8,128)(2,1)S(1)} all-to-all(bf16[16,80,3072]{2,1,0:T(8,128)(2,1)S(1)} %bitcast.48), channel_id=1, replica_groups=mesh['worker'=16,'expert'=16] {'expert'}, dimensions={0} | all-to-all | bytes 15728640 | tf_op jit(solution)/shard_map/all_to_all | solution.py:72
  209.9 2.3 fusion.15
  213.1 3.5 multiply_convert_fusion.3
  216.6 5.3 convolution_convert_fusion
  221.9 7.0 all-to-all-start.1
  229.7 173.6 %all-to-all-done.1 = bf16[16,80,3072]{2,1,0:T(8,128)(2,1)} async-done(((bf16[16,80,3072]{2,1,0:T(8,128)(2,1)}), bf16[16,80,3072]{2,1,0:T(8,128)(2,1)}, u32[]{:S(2)}, u32[]{:S(2)}) %all-to-all-start.1) | async-done | bytes 7864352 | tf_op jit(solution)/shard_map/all_to_all | solution.py:77
  403.3 7.1 convert_reduce_fusion
  410.4 6.9 gather_fusion.1
  417.3 5.2 gather.21
  422.5 7.7 multiply_reduce_fusion
  430.6 2.8 mul.106
  433.4 5.2 mul.107
  438.7 2.2 multiply_convert_fusion
  440.9 3.4 gather_fusion.2
  444.3 1.9 select_select_fusion
  446.2 4.1 broadcast_in_dim.78
  450.3 5.0 all-to-all-start.2
  456.1 168.2 %all-to-all-done.2 = bf16[16,80,3072]{2,1,0:T(8,128)(2,1)} async-done(((bf16[16,80,3072]{2,1,0:T(8,128)(2,1)}), bf16[16,80,3072]{2,1,0:T(8,128)(2,1)}, u32[]{:S(2)}, u32[]{:S(2)}) %all-to-all-start.2) | async-done | bytes 7864352 | tf_op jit(solution)/shard_map/all_to_all | solution.py:103
  624.3 7.6 fusion.2
  632.0 5.6 fusion.16
  638.6 6.9 fusion.1
  645.6 7.7 fusion
  653.3 40.4 %psum.7 = f32[]{:T(128)} all-reduce(f32[]{:T(128)} %bitcast), channel_id=1, replica_groups=mesh['worker'=16,'expert'=16] {'worker'}, use_global_device_ids=true, to_apply=%region_7.8 | all-reduce | flops 1 | bytes 8 | tf_op jit(solution)/shard_map/psum | solution.py:106
  694.3 12.8 %reduce-scatter.8.cloned.1.call-done = bf16[256,192]{0,1:T(8,128)(2,1)} async-done(((bf16[256,3072]{0,1:T(8,128)(2,1)}), bf16[256,192]{0,1:T(8,128)(2,1)}) %reduce-scatter.8.cloned.1.call-update) | async-done | bytes 98320 | tf_op jit(solution)/shard_map/reduce_scatter | solution.py:118
  707.1 2.1 convert_divide_fusion
  709.2 64.6 %reduce-scatter.6.cloned.1.call-done = bf16[192,256]{1,0:T(8,128)(2,1)} async-done(((bf16[3072,256]{1,0:T(8,128)(2,1)}), bf16[192,256]{1,0:T(8,128)(2,1)}) %reduce-scatter.6.cloned.1.call-update) | async-done | bytes 98320 | tf_op jit(solution)/shard_map/reduce_scatter | solution.py:115
  773.9 2.1 convert_divide_fusion.1
  776.0 64.6 %reduce-scatter.4.cloned.1.call-done = bf16[192,256]{1,0:T(8,128)(2,1)} async-done(((bf16[3072,256]{1,0:T(8,128)(2,1)}), bf16[192,256]{1,0:T(8,128)(2,1)}) %reduce-scatter.4.cloned.1.call-update) | async-done | bytes 98320 | tf_op jit(solution)/shard_map/reduce_scatter | solution.py:112
  840.7 2.1 convert_divide_fusion.2
  (68 shorter events, 10.2 us)
Async XLA Ops:
  7.2 209.4 %copy-start = (bf16[256,3072]{1,0:T(8,128)(2,1)S(1)}, bf16[256,3072]{1,0:T(8,128)(2,1)}, u32[]{:S(2)}) copy-start(bf16[256,3072]{1,0:T(8,128)(2,1)} %param.15) | copy-start | bytes 4718596
  23.4 186.5 %copy-start.9 = (bf16[3072,256]{1,0:T(8,128)(2,1)S(1)}, bf16[3072,256]{1,0:T(8,128)(2,1)}, u32[]{:S(2)}) copy-start(bf16[3072,256]{1,0:T(8,128)(2,1)} %param.13) | copy-start | bytes 4718596
  209.9 3.2 copy-start.1
  209.9 3.2 copy-start.10
  213.1 3.5 copy-start.11
  216.6 5.3 copy-start.2
  221.9 7.2 copy-start.5
  221.9 7.4 copy-start.7
  221.9 7.6 copy-start.8
  221.9 181.4 %all-to-all-start.1 = ((bf16[16,80,3072]{2,1,0:T(8,128)(2,1)}), bf16[16,80,3072]{2,1,0:T(8,128)(2,1)}, u32[]{:S(2)}, u32[]{:S(2)}) async-start(bf16[16,80,3072]{2,1,0:T(8,128)(2,1)} %bitcast.46), calls=%async_computation.1 | async-start | bytes 15728640 | tf_op jit(solution)/shard_map/all_to_all | solution.py:77
  422.5 7.8 copy-start.4
  440.9 3.4 copy-start.6
  450.3 174.1 %copy-start.3 = (bf16[1280,256]{1,0:T(8,128)(2,1)S(1)}, bf16[1280,256]{1,0:T(8,128)(2,1)}, u32[]{:S(2)}) copy-start(bf16[1280,256]{1,0:T(8,128)(2,1)} %copy-done.2) | copy-start | bytes 1966084
  450.3 174.1 %all-to-all-start.2 = ((bf16[16,80,3072]{2,1,0:T(8,128)(2,1)}), bf16[16,80,3072]{2,1,0:T(8,128)(2,1)}, u32[]{:S(2)}, u32[]{:S(2)}) async-start(bf16[16,80,3072]{2,1,0:T(8,128)(2,1)} %bitcast.47), calls=%async_computation.2 | async-start | bytes 15728640 | tf_op jit(solution)/shard_map/all_to_all | solution.py:103
  455.2 251.9 %reduce-scatter.8.cloned.1.call-start = ((), (), s32[]{:S(2)}) async-start(), calls=%async_computation.8 | async-start | bytes 1671168 | tf_op jit(solution)/shard_map/reduce_scatter | solution.py:118
  631.9 6.7 copy-start.12
  631.9 141.9 %reduce-scatter.6.cloned.1.call-start = ((), (), s32[]{:S(2)}) async-start(), calls=%async_computation.7 | async-start | bytes 1671168 | tf_op jit(solution)/shard_map/reduce_scatter | solution.py:115
  637.6 1.1 copy-start.13
  645.5 195.1 %reduce-scatter.4.cloned.1.call-start = ((), (), s32[]{:S(2)}) async-start(), calls=%async_computation.6 | async-start | bytes 1671168 | tf_op jit(solution)/shard_map/reduce_scatter | solution.py:112
Sparse Core Ops, SparseCore 0:
  632.1 74.9 reduce-scatter.7
  709.6 64.2 reduce-scatter.5
  776.4 64.2 reduce-scatter.3
where the time goes:
time: 855 us; the launch traced here: 850 us
  waiting for transfers between devices  484 us (57%)
  blocking collectives  227 us (27%)
  local copies, waits for them, and re-layouts  42.9 us (5%)
  matrix products  38.8 us (5%)
  other arithmetic  29.8 us (3%)
  between operations  14.9 us (2%)
  starting transfers between devices  12.3 us (1%)
    all_to_all x1, blocking collectives, per_device(): lax.all_to_all(send_tokens, 'expert', split_axis=0, concat_axis=0, tiled=...  187 us
    all_to_all x1, waiting for transfers between devices, per_device(): lax.all_to_all(partial_slots.reshape(expert_devices, CAP, width), 'expert...  174 us
    all_to_all x1, waiting for transfers between devices, per_device(): lax.all_to_all(send_cot, 'expert', split_axis=0, concat_axis=0, tiled=True)  168 us
    reduce_scatter x1, waiting for transfers between devices, per_device(): lax.psum_scatter((weight * gate_grad).astype(jnp.bfloat16), 'worker', sca...  64.6 us
    reduce_scatter x1, waiting for transfers between devices, per_device(): lax.psum_scatter((weight * up_grad).astype(jnp.bfloat16), 'worker', scatt...  64.6 us
    psum x1, blocking collectives, per_device(): total_steps = lax.psum(weight, 'worker')  40.4 us
    dot_general x3, matrix products, contract_rows(): lax.dot_general(left, right, (((0,), (0,)), ((), ())), preferred_element_...  22.2 us
  transfers between devices with their start and end apart: 5, of which 5 were waited for; matrix products, arithmetic and copies ran while one was open for 3% of the time, Pallas kernels for 0%

commit v1 on v0

--- a/solution.py
+++ b/solution.py
@@ -5,6 +5,10 @@
 
 EXPERTS = 4
 CAP = 80
+
+
+def ends_set(view):
+    return jnp.sum(jax.lax.all_gather(view, "worker"), axis=0)
 
 
 def silu_parts(pre):
@@ -103,7 +107,7 @@
     cot_arrived = lax.all_to_all(send_cot, "expert", split_axis=0, concat_axis=0, tiled=True)
     cot_slots = cot_arrived.reshape(slot_total, width)
     weight = step_count[0].astype(jnp.float32)
-    total_steps = lax.psum(weight, "worker")
+    total_steps = ends_set(weight)
     grad_gate, grad_up = hidden_grads(cot_slots, gate_pre, up_pre, down_weight)
     down_grad, grad_gate, grad_up = (contract_rows(hidden, cot_slots), grad_gate, grad_up)
     gate_grad = contract_rows(expert_rows, grad_gate)

time: 855 us -> 855 us (level)
    psum x1 -> x0, blocking collectives: 40.4 us -> none  [per_device(): total_steps = lax.psum(weight, 'worker')]
    unnamed x0 -> x1, blocking collectives: none -> 39.3 us
where the time goes in v1:
time: 855 us; the launch traced here: 850 us
  waiting for transfers between devices  483 us (56%)
  blocking collectives  226 us (26%)
  local copies, waits for them, and re-layouts  43.5 us (5%)
  matrix products  38.9 us (5%)
  other arithmetic  31.1 us (4%)
  between operations  14.9 us (2%)
  starting transfers between devices  12.3 us (1%)
    all_to_all x1, blocking collectives, per_device(): lax.all_to_all(send_tokens, 'expert', split_axis=0, concat_axis=0, tiled=...  187 us
    all_to_all x1, waiting for transfers between devices, per_device(): lax.all_to_all(partial_slots.reshape(expert_devices, CAP, width), 'expert...  174 us
    all_to_all x1, waiting for transfers between devices, per_device(): lax.all_to_all(send_cot, 'expert', split_axis=0, concat_axis=0, tiled=True)  168 us
    reduce_scatter x1, waiting for transfers between devices, per_device(): lax.psum_scatter((weight * up_grad).astype(jnp.bfloat16), 'worker', scatt...  64.8 us
    reduce_scatter x1, waiting for transfers between devices, per_device(): lax.psum_scatter((weight * gate_grad).astype(jnp.bfloat16), 'worker', sca...  64.6 us
    unnamed x1, blocking collectives  39.3 us
    dot_general x3, matrix products, contract_rows(): lax.dot_general(left, right, (((0,), (0,)), ((), ())), preferred_element_...  22.2 us
  transfers between devices with their start and end apart: 5, of which 5 were waited for; matrix products, arithmetic and copies ran while one was open for 3% of the time, Pallas kernels for 0%

profile of v1, /device:TPU:4, one launch (start us, length us, event | category | flops | bytes accessed | tf_op | source)
XLA Modules:
  0.0 849.8 jit_solution(5556390066564996712)
XLA Ops:
  9.1 1.2 reduce-window.6
  11.0 1.4 scatter_custom_fusion
  14.1 7.3 gather_fusion
  23.4 186.5 %all_to_all.15 = bf16[16,80,3072]{2,1,0:T(8,128)(2,1)S(1)} all-to-all(bf16[16,80,3072]{2,1,0:T(8,128)(2,1)S(1)} %bitcast.49), channel_id=1, replica_groups=mesh['worker'=16,'expert'=16] {'expert'}, dimensions={0} | all-to-all | bytes 15728640 | tf_op jit(solution)/shard_map/all_to_all | solution.py:76
  209.9 2.3 fusion.15
  213.1 3.5 multiply_convert_fusion.3
  216.6 5.3 convolution_convert_fusion
  221.9 7.0 all-to-all-start.1
  229.7 173.6 %all-to-all-done.1 = bf16[16,80,3072]{2,1,0:T(8,128)(2,1)} async-done(((bf16[16,80,3072]{2,1,0:T(8,128)(2,1)}), bf16[16,80,3072]{2,1,0:T(8,128)(2,1)}, u32[]{:S(2)}, u32[]{:S(2)}) %all-to-all-start.1) | async-done | bytes 7864352 | tf_op jit(solution)/shard_map/all_to_all | solution.py:81
  403.3 7.1 convert_reduce_fusion
  410.4 6.9 gather_fusion.1
  417.3 5.2 gather.21
  422.5 7.7 multiply_reduce_fusion
  430.6 2.8 mul.106
  433.4 5.2 mul.107
  438.7 2.2 multiply_convert_fusion
  440.9 3.4 gather_fusion.2
  444.3 1.9 select_select_fusion
  446.2 4.1 broadcast_in_dim.78
  450.3 5.0 all-to-all-start.2
  456.1 168.2 %all-to-all-done.2 = bf16[16,80,3072]{2,1,0:T(8,128)(2,1)} async-done(((bf16[16,80,3072]{2,1,0:T(8,128)(2,1)}), bf16[16,80,3072]{2,1,0:T(8,128)(2,1)}, u32[]{:S(2)}, u32[]{:S(2)}) %all-to-all-start.2) | async-done | bytes 7864352 | tf_op jit(solution)/shard_map/all_to_all | solution.py:107
  624.3 7.6 fusion.2
  632.0 5.6 fusion.16
  638.6 6.9 fusion.1
  645.6 7.7 fusion
  654.7 39.3 %all-reduce = f32[16]{0:T(128)S(1)} all-reduce(f32[16]{0:T(128)S(1)} %convert_dynamic-update-slice_fusion), channel_id=1, replica_groups=mesh['worker'=16,'expert'=16] {'worker'}, use_global_device_ids=true, to_apply=%add | all-reduce | flops 16 | bytes 128
  695.2 11.9 %reduce-scatter.8.cloned.1.call-done = bf16[256,192]{0,1:T(8,128)(2,1)} async-done(((bf16[256,3072]{0,1:T(8,128)(2,1)}), bf16[256,192]{0,1:T(8,128)(2,1)}) %reduce-scatter.8.cloned.1.call-update) | async-done | bytes 98320 | tf_op jit(solution)/shard_map/reduce_scatter | solution.py:122
  707.1 2.1 convert_divide_fusion
  709.3 64.8 %reduce-scatter.6.cloned.1.call-done = bf16[192,256]{1,0:T(8,128)(2,1)} async-done(((bf16[3072,256]{1,0:T(8,128)(2,1)}), bf16[192,256]{1,0:T(8,128)(2,1)}) %reduce-scatter.6.cloned.1.call-update) | async-done | bytes 98320 | tf_op jit(solution)/shard_map/reduce_scatter | solution.py:119
  774.1 2.1 convert_divide_fusion.1
  776.2 64.6 %reduce-scatter.4.cloned.1.call-done = bf16[192,256]{1,0:T(8,128)(2,1)} async-done(((bf16[3072,256]{1,0:T(8,128)(2,1)}), bf16[192,256]{1,0:T(8,128)(2,1)}) %reduce-scatter.4.cloned.1.call-update) | async-done | bytes 98320 | tf_op jit(solution)/shard_map/reduce_scatter | solution.py:116
  840.9 2.1 convert_divide_fusion.2
  (74 shorter events, 12.1 us)
Async XLA Ops:
  7.2 209.4 %copy-start = (bf16[256,3072]{1,0:T(8,128)(2,1)S(1)}, bf16[256,3072]{1,0:T(8,128)(2,1)}, u32[]{:S(2)}) copy-start(bf16[256,3072]{1,0:T(8,128)(2,1)} %param.15) | copy-start | bytes 4718596
  23.4 186.5 %copy-start.9 = (bf16[3072,256]{1,0:T(8,128)(2,1)S(1)}, bf16[3072,256]{1,0:T(8,128)(2,1)}, u32[]{:S(2)}) copy-start(bf16[3072,256]{1,0:T(8,128)(2,1)} %param.13) | copy-start | bytes 4718596
  209.9 3.2 copy-start.1
  209.9 3.2 copy-start.10
  213.1 3.5 copy-start.12
  216.6 5.3 copy-start.2
  221.9 7.2 copy-start.5
  221.9 7.4 copy-start.7
  221.9 7.6 copy-start.8
  221.9 181.4 %all-to-all-start.1 = ((bf16[16,80,3072]{2,1,0:T(8,128)(2,1)}), bf16[16,80,3072]{2,1,0:T(8,128)(2,1)}, u32[]{:S(2)}, u32[]{:S(2)}) async-start(bf16[16,80,3072]{2,1,0:T(8,128)(2,1)} %bitcast.47), calls=%async_computation.1 | async-start | bytes 15728640 | tf_op jit(solution)/shard_map/all_to_all | solution.py:81
  422.5 7.8 copy-start.4
  440.9 3.4 copy-start.6
  450.3 174.1 %copy-start.3 = (bf16[1280,256]{1,0:T(8,128)(2,1)S(1)}, bf16[1280,256]{1,0:T(8,128)(2,1)}, u32[]{:S(2)}) copy-start(bf16[1280,256]{1,0:T(8,128)(2,1)} %copy-done.2) | copy-start | bytes 1966084
  450.3 174.1 %all-to-all-start.2 = ((bf16[16,80,3072]{2,1,0:T(8,128)(2,1)}), bf16[16,80,3072]{2,1,0:T(8,128)(2,1)}, u32[]{:S(2)}, u32[]{:S(2)}) async-start(bf16[16,80,3072]{2,1,0:T(8,128)(2,1)} %bitcast.48), calls=%async_computation.2 | async-start | bytes 15728640 | tf_op jit(solution)/shard_map/all_to_all | solution.py:107
  455.2 251.9 %reduce-scatter.8.cloned.1.call-start = ((), (), s32[]{:S(2)}) async-start(), calls=%async_computation.8 | async-start | bytes 1671168 | tf_op jit(solution)/shard_map/reduce_scatter | solution.py:122
  631.9 6.7 copy-start.13
  631.9 142.2 %reduce-scatter.6.cloned.1.call-start = ((), (), s32[]{:S(2)}) async-start(), calls=%async_computation.7 | async-start | bytes 1671168 | tf_op jit(solution)/shard_map/reduce_scatter | solution.py:119
  637.6 1.1 copy-start.14
  645.6 195.3 %reduce-scatter.4.cloned.1.call-start = ((), (), s32[]{:S(2)}) async-start(), calls=%async_computation.6 | async-start | bytes 1671168 | tf_op jit(solution)/shard_map/reduce_scatter | solution.py:116
  645.6 7.8 copy-start.11
Sparse Core Ops, SparseCore 0:
  632.1 75.0 reduce-scatter.7
  709.6 64.4 reduce-scatter.5
  776.6 64.2 reduce-scatter.3
